TPU v7x, 32 devices: a whole 2x2x4 slice. The times are simulated.
32 devices in a mesh: item: 8 (over z, y), code: 4 (over x, core).
Axes of the slice: x: 2, y: 2, z: 4, core: 2. Of those that a mesh axis runs over, the one named last changes fastest.
Arguments:
- residuals: float32 [256, 32768], P('code', 'item'), may hold values from -6 to 6
- codebook: float32 [256, 32768], P('item', 'code'), may hold values from -6 to 6
- item_weight: float32 [32768], P('item'), may hold values from 1 to 100
- code_capacity: float32 [32768], P('code'), may hold values from 0.25 to 4
- pairs: int32 [512, 64], P('item', 'code'), may hold values from -1 to 127, as said below
Outputs:
- item_potential: float32 [32768], P('item')
- code_potential: float32 [32768], P('code')
Inputs may be any that keep to these rules, and one draw needn't show every extreme that they name: `pairs`: each entry is -1 (no candidate) or a code block's number within the code shard of its slot column. Within one item block and one code shard the live entries are distinct, the first slot is always live, and between 1 and 8 are live; some device holds exactly 8 live slots in every item block. Every code block is named by some item block.
All inputs are finite; a program needn't handle non-finite values.
Results may differ from a plain program's by a relative error of at most 0.0003.
Values sent between devices are 32-bit elements; how exact they have to be, the bound alone decides.
No kernel may reach another device: no remote copies, remote signals or barrier semaphores. Data moves between devices by JAX's collectives and lax.ppermute only.
A program may use at most 128 MiB of HBM per device.

v0:
```python
import math
import jax
import jax.numpy as jnp
from jax import lax
from jax.sharding import PartitionSpec as P

BLOCK = 64
ITERS = 3
masked_score = -1e30
softness_factor = 0.1


def body(residuals, codebook, item_weight, code_capacity, pairs):
    item_columns = lax.all_gather(residuals, "code", axis=0, tiled=True)
    code_cols = lax.all_gather(codebook, "item", axis=0, tiled=True)
    embedding_width = item_columns.shape[0]
    item_count = item_columns.shape[1]
    code_count = code_cols.shape[1]
    item_blocks = item_count // BLOCK
    code_blocks = code_count // BLOCK
    logit_scale = 1.0 / (softness_factor * math.sqrt(embedding_width))
    weight_sum = lax.psum(jnp.sum(item_weight), "item")
    capacity_sum = lax.psum(jnp.sum(code_capacity), "code")
    item_logmass = jnp.log(item_weight) - jnp.log(weight_sum)
    code_logmass = jnp.log(code_capacity) - jnp.log(capacity_sum)
    slot_order = jnp.argsort((pairs < 0).astype(jnp.int32), axis=1, stable=True)[
        :, : pairs.shape[1] // 2
    ]
    chosen = jnp.take_along_axis(pairs, slot_order, axis=1)
    is_live = chosen >= 0
    safe_ids = jnp.where(is_live, chosen, 0)
    target = jnp.where(is_live, chosen, code_blocks)
    item_split_cols = item_columns.reshape(embedding_width, item_blocks, BLOCK)
    code_column_splits = code_cols.reshape(embedding_width, code_blocks, BLOCK)
    group = math.gcd(item_blocks, 8)
    group_count = item_blocks // group

    def build_tiles(own, ids, live):
        picked = code_column_splits[:, ids, :]
        scores = (
            jnp.einsum("rbi,rbsj->bsij", own, picked, precision=lax.Precision.HIGHEST) * logit_scale
        )
        return jnp.where(live[:, :, None, None], scores, masked_score)

    reduce_fn = lambda tiles, ids, portion: tiles

    def one_group(group_index):
        start = group_index * group
        own = lax.dynamic_slice_in_dim(item_split_cols, start, group, 1)
        ids = lax.dynamic_slice_in_dim(safe_ids, start, group, 0)
        live = lax.dynamic_slice_in_dim(is_live, start, group, 0)
        portion = lax.dynamic_slice_in_dim(safe_ids, start, group, 0)
        return reduce_fn(build_tiles(own, ids, live), ids, portion)

    results = lax.map(one_group, jnp.arange(group_count, dtype=jnp.int32))
    saved_tile_blocks = results.reshape((item_blocks,) + results.shape[2:])

    def run_pass(reduce_fn, extra):
        return reduce_fn(saved_tile_blocks, safe_ids, extra)

    flat_target = target.reshape(-1)
    flat_rows = flat_target.shape[0]
    row_group = math.gcd(flat_rows, 256)
    one_hot = flat_target[:, None] == jnp.arange(code_blocks, dtype=jnp.int32)[None, :]
    one_hot_groups = one_hot.reshape(flat_rows // row_group, row_group, code_blocks)
    one_hot_float = one_hot.astype(jnp.float32)
    code_potential = jnp.zeros((code_count,), jnp.float32)
    item_potential = jnp.zeros((item_count,), jnp.float32)
    for sweep in range(ITERS):
        code_split = code_potential.reshape(code_blocks, BLOCK)

        def row_reduce(tiles, ids, portion):
            logits = tiles + code_split[ids][:, :, None, :]
            block_peak = jnp.max(logits, axis=(1, 3))
            block_total = jnp.sum(jnp.exp(logits - block_peak[:, None, :, None]), axis=(1, 3))
            return (block_peak, block_total)

        row_peak, row_total = run_pass(row_reduce, safe_ids)
        row_peak = row_peak.reshape(item_count)
        row_total = row_total.reshape(item_count)
        merged_peak = lax.pmax(row_peak, "code")
        merged_total = lax.psum(row_total * jnp.exp(row_peak - merged_peak), "code")
        item_potential = item_logmass - (merged_peak + jnp.log(merged_total))
        item_split = item_potential.reshape(item_blocks, BLOCK)

        def col_reduce(tiles, ids, portion):
            logits = tiles + portion[:, None, :, None]
            block_peak = jnp.max(logits, axis=2)
            block_total = jnp.sum(jnp.exp(logits - block_peak[:, :, None, :]), axis=2)
            return (block_peak, block_total)

        tile_peak, tile_total = run_pass(col_reduce, item_split)
        peak_flat = tile_peak.reshape(flat_rows, BLOCK)
        total_flat = tile_total.reshape(flat_rows, BLOCK)
        peak_groups = peak_flat.reshape(flat_rows // row_group, row_group, BLOCK)

        def peak_step(carry, pieces):
            hot, peaks = pieces
            candidate = jnp.max(jnp.where(hot[:, :, None], peaks[:, None, :], masked_score), axis=0)
            return (jnp.maximum(carry, candidate), None)

        col_peak, unused = lax.scan(
            peak_step,
            jnp.full((code_blocks, BLOCK), masked_score, jnp.float32),
            (one_hot_groups, peak_groups),
        )
        padded_peak = jnp.concatenate(
            [col_peak, jnp.full((1, BLOCK), masked_score, jnp.float32)], axis=0
        )
        spread = total_flat * jnp.exp(peak_flat - padded_peak[flat_target])
        col_total = jnp.dot(
            one_hot_float.T,
            spread,
            precision=lax.Precision.HIGHEST,
            preferred_element_type=jnp.float32,
        )
        col_peak = col_peak.reshape(code_count)
        col_total = col_total.reshape(code_count)
        joined_peak = lax.pmax(col_peak, "item")
        joined_total = lax.psum(col_total * jnp.exp(col_peak - joined_peak), "item")
        code_potential = code_logmass - (joined_peak + jnp.log(joined_total))
    return (item_potential, code_potential)


def solution(mesh):
    placed = (P("code", "item"), P("item", "code"), P("item"), P("code"), P("item", "code"))
    return jax.shard_map(
        body, mesh=mesh, in_specs=placed, out_specs=(P("item"), P("code")), check_vma=False
    )
```

profile of v0, /device:TPU:0, one launch (start us, length us, event | category | flops | bytes accessed | tf_op | source)
XLA Modules:
  0.0 706.6 jit_solution(5821192888771860012)
XLA Ops:
  8.7 1.3 reduce_sum.72
  10.0 23.8 %psum.56 = f32[]{:T(128)} all-reduce(f32[]{:T(128)} %reduce_sum.72), channel_id=1, replica_groups=mesh['item'=8,'code'=4] {'item'}, use_global_device_ids=true, to_apply=%region_1.0 | all-reduce | flops 1 | bytes 8 | tf_op jit(solution)/shard_map/psum | solution.py:22
  35.4 3.9 gather_fusion.7
  41.4 1.0 gather_fusion.1
  42.6 4.1 all-gather.5.cloned.1.call-done
  46.8 5.6 copy.38
  52.4 121.0 %all-gather.3.cloned.1.call-done = f32[256,8192]{1,0:T(8,128)} async-done(((f32[32,8192]{1,0:T(8,128)}), f32[256,8192]{1,0:T(8,128)}) %all-gather.3.cloned.1.call-update) | async-done | bytes 8388624 | tf_op jit(solution)/shard_map/all_gather | solution.py:15
  173.4 9.0 %copy.37 = f32[256,8192]{0,1:T(8,128)} copy(f32[256,8192]{1,0:T(8,128)} %all-gather.3.cloned.1.call-done) | data formatting | bytes 16777216 | tf_op jit(solution)/shard_map/all_gather | solution.py:15
  182.4 120.6 %while.43 = (s32[]{:T(128)}, f32[8,8,8,64,64]{3,4,2,1,0:T(8,128)}, s32[8]{0:T(128)S(1)}, pred[64,8]{0,1:T(8,128)(4,1)S(1)}, s32[64,8]{0,1:T(8,128)S(1)}, /*index...) while((s32[]{:T(128)}, f32[8,8,8,64,64]{3,4,2,1,0:T(8,128)}, ...), condition=%wide.region_4.0_spmd, body=%wide.region_3.0_spmd.sunk | while | flops 805831872 | bytes 15212019 | solution.py:55
  183.9 6.2 gather_fusion
  190.2 7.3 %bitcast_dynamic-update-slice_fusion.2 = f32[8,8,8,64,64]{3,4,2,1,0:T(8,128)} fusion(f32[8,8,8,64,64]{3,4,2,1,0:T(8,128)} %get-tuple-element.349, s32[]{:T(128)} %get-tuple-element.348, f32[256,8,8,64]{0,3,2,1:T(8,128)} %bitcast.88, pred[8,8]{1,0:T(8,128)(4,1)S(1)} %copy.63, f32[256,64,64]{0,2,1:T(8,128)} %get-tuple-element.365, s32[]{:T(128)S(6)} %select_n.148), kind=kOutput, calls=%fused_computation.8.clone.1 | convolution fusion | flops 805830656 | bytes 6816324 | tf_op jit(solution)/shard_map/while/body/eval_jaxpr/rbi,rbsj->bsij/dot_general | solution.py:41
  199.0 6.2 gather_fusion
  205.3 7.2 %bitcast_dynamic-update-slice_fusion.2 = f32[8,8,8,64,64]{3,4,2,1,0:T(8,128)} fusion(f32[8,8,8,64,64]{3,4,2,1,0:T(8,128)} %get-tuple-element.349, s32[]{:T(128)} %get-tuple-element.348, f32[256,8,8,64]{0,3,2,1:T(8,128)} %bitcast.88, pred[8,8]{1,0:T(8,128)(4,1)S(1)} %copy.63, f32[256,64,64]{0,2,1:T(8,128)} %get-tuple-element.365, s32[]{:T(128)S(6)} %select_n.148), kind=kOutput, calls=%fused_computation.8.clone.1 | convolution fusion | flops 805830656 | bytes 6816324 | tf_op jit(solution)/shard_map/while/body/eval_jaxpr/rbi,rbsj->bsij/dot_general | solution.py:41
  214.0 6.2 gather_fusion
  220.3 7.3 %bitcast_dynamic-update-slice_fusion.2 = f32[8,8,8,64,64]{3,4,2,1,0:T(8,128)} fusion(f32[8,8,8,64,64]{3,4,2,1,0:T(8,128)} %get-tuple-element.349, s32[]{:T(128)} %get-tuple-element.348, f32[256,8,8,64]{0,3,2,1:T(8,128)} %bitcast.88, pred[8,8]{1,0:T(8,128)(4,1)S(1)} %copy.63, f32[256,64,64]{0,2,1:T(8,128)} %get-tuple-element.365, s32[]{:T(128)S(6)} %select_n.148), kind=kOutput, calls=%fused_computation.8.clone.1 | convolution fusion | flops 805830656 | bytes 6816324 | tf_op jit(solution)/shard_map/while/body/eval_jaxpr/rbi,rbsj->bsij/dot_general | solution.py:41
  229.0 6.2 gather_fusion
  235.4 7.3 %bitcast_dynamic-update-slice_fusion.2 = f32[8,8,8,64,64]{3,4,2,1,0:T(8,128)} fusion(f32[8,8,8,64,64]{3,4,2,1,0:T(8,128)} %get-tuple-element.349, s32[]{:T(128)} %get-tuple-element.348, f32[256,8,8,64]{0,3,2,1:T(8,128)} %bitcast.88, pred[8,8]{1,0:T(8,128)(4,1)S(1)} %copy.63, f32[256,64,64]{0,2,1:T(8,128)} %get-tuple-element.365, s32[]{:T(128)S(6)} %select_n.148), kind=kOutput, calls=%fused_computation.8.clone.1 | convolution fusion | flops 805830656 | bytes 6816324 | tf_op jit(solution)/shard_map/while/body/eval_jaxpr/rbi,rbsj->bsij/dot_general | solution.py:41
  244.1 6.2 gather_fusion
  250.4 7.3 %bitcast_dynamic-update-slice_fusion.2 = f32[8,8,8,64,64]{3,4,2,1,0:T(8,128)} fusion(f32[8,8,8,64,64]{3,4,2,1,0:T(8,128)} %get-tuple-element.349, s32[]{:T(128)} %get-tuple-element.348, f32[256,8,8,64]{0,3,2,1:T(8,128)} %bitcast.88, pred[8,8]{1,0:T(8,128)(4,1)S(1)} %copy.63, f32[256,64,64]{0,2,1:T(8,128)} %get-tuple-element.365, s32[]{:T(128)S(6)} %select_n.148), kind=kOutput, calls=%fused_computation.8.clone.1 | convolution fusion | flops 805830656 | bytes 6816324 | tf_op jit(solution)/shard_map/while/body/eval_jaxpr/rbi,rbsj->bsij/dot_general | solution.py:41
  259.2 6.2 gather_fusion
  265.6 7.2 %bitcast_dynamic-update-slice_fusion.2 = f32[8,8,8,64,64]{3,4,2,1,0:T(8,128)} fusion(f32[8,8,8,64,64]{3,4,2,1,0:T(8,128)} %get-tuple-element.349, s32[]{:T(128)} %get-tuple-element.348, f32[256,8,8,64]{0,3,2,1:T(8,128)} %bitcast.88, pred[8,8]{1,0:T(8,128)(4,1)S(1)} %copy.63, f32[256,64,64]{0,2,1:T(8,128)} %get-tuple-element.365, s32[]{:T(128)S(6)} %select_n.148), kind=kOutput, calls=%fused_computation.8.clone.1 | convolution fusion | flops 805830656 | bytes 6816324 | tf_op jit(solution)/shard_map/while/body/eval_jaxpr/rbi,rbsj->bsij/dot_general | solution.py:41
  274.3 6.2 gather_fusion
  280.6 7.3 %bitcast_dynamic-update-slice_fusion.2 = f32[8,8,8,64,64]{3,4,2,1,0:T(8,128)} fusion(f32[8,8,8,64,64]{3,4,2,1,0:T(8,128)} %get-tuple-element.349, s32[]{:T(128)} %get-tuple-element.348, f32[256,8,8,64]{0,3,2,1:T(8,128)} %bitcast.88, pred[8,8]{1,0:T(8,128)(4,1)S(1)} %copy.63, f32[256,64,64]{0,2,1:T(8,128)} %get-tuple-element.365, s32[]{:T(128)S(6)} %select_n.148), kind=kOutput, calls=%fused_computation.8.clone.1 | convolution fusion | flops 805830656 | bytes 6816324 | tf_op jit(solution)/shard_map/while/body/eval_jaxpr/rbi,rbsj->bsij/dot_general | solution.py:41
  289.4 6.2 gather_fusion
  295.7 7.3 %bitcast_dynamic-update-slice_fusion.2 = f32[8,8,8,64,64]{3,4,2,1,0:T(8,128)} fusion(f32[8,8,8,64,64]{3,4,2,1,0:T(8,128)} %get-tuple-element.349, s32[]{:T(128)} %get-tuple-element.348, f32[256,8,8,64]{0,3,2,1:T(8,128)} %bitcast.88, pred[8,8]{1,0:T(8,128)(4,1)S(1)} %copy.63, f32[256,64,64]{0,2,1:T(8,128)} %get-tuple-element.365, s32[]{:T(128)S(6)} %select_n.148), kind=kOutput, calls=%fused_computation.8.clone.1 | convolution fusion | flops 805830656 | bytes 6816324 | tf_op jit(solution)/shard_map/while/body/eval_jaxpr/rbi,rbsj->bsij/dot_general | solution.py:41
  302.9 9.4 %add_reduce_fusion.5 = f32[8,8,64]{2,1,0:T(8,128)S(1)} fusion(f32[8,8,8,64,64]{3,4,2,1,0:T(8,128)} %get-tuple-element.107, f32[8,8,8,64]{3,2,1,0:T(8,128)S(1)} %bitcast.97), kind=kLoop, calls=%fused_computation.39 | loop fusion | flops 4190208 | bytes 8536064 | tf_op jit(solution)/shard_map/reduce_max | solution.py:74
  312.3 1.3 copy-done.1
  313.7 5.1 exponential_reduce_fusion.5
  319.0 10.2 %pmax.42 = f32[4096]{0:T(1024)S(1)} all-reduce(f32[4096]{0:T(1024)S(1)} %reshape.247), channel_id=1, replica_groups=mesh['item'=8,'code'=4] {'code'}, use_global_device_ids=true, to_apply=%region_8.9 | all-reduce | flops 4096 | bytes 32768 | tf_op jit(solution)/shard_map/pmax | solution.py:81
  329.2 11.4 %all-reduce.3 = (f32[4096]{0:T(1024)S(1)}, f32[]{:T(128)}) all-reduce(f32[4096]{0:T(1024)S(1)} %exponential_multiply_fusion.5, f32[]{:T(128)} %reduce_sum.73), channel_id=1, replica_groups=mesh['item'=8,'code'=4] {'code'}, use_global_device_ids=true, to_apply=%region_10.11 | all-reduce | flops 4097 | bytes 32776 | tf_op jit(solution)/shard_map/psum | solution.py:82
  340.7 8.2 %add_reduce_fusion.4 = f32[8,8,8,64]{3,2,1,0:T(8,128)S(1)} fusion(f32[8,8,8,64,64]{3,4,2,1,0:T(8,128)} %get-tuple-element.107, f32[8,8,64]{2,1,0:T(8,128)S(1)} %add.166), kind=kLoop, calls=%fused_computation.38 | loop fusion | flops 4161536 | bytes 8536064 | tf_op jit(solution)/shard_map/reduce_max | solution.py:88
  348.9 11.1 %exponential_reduce_fusion.4 = f32[8,8,8,64]{3,2,1,0:T(8,128)S(1)} fusion(f32[8,8,8,64,64]{3,4,2,1,0:T(8,128)} %get-tuple-element.107, f32[8,8,8,64]{3,2,1,0:T(8,128)S(1)} %add_reduce_fusion.4, f32[8,8,64]{2,1,0:T(8,128)S(1)} %add.166), kind=kLoop, calls=%fused_computation.32 | loop fusion | flops 6258688 | bytes 8667136 | tf_op jit(solution)/shard_map/reduce_sum | solution.py:89
  359.9 6.7 while.44
  360.0 3.2 select_reduce_fusion.6
  363.3 3.2 select_reduce_fusion.6
  366.8 1.0 gather_fusion.2
  368.5 35.2 %pmax.43 = f32[8192]{0:T(1024)S(1)} all-reduce(f32[8192]{0:T(1024)S(1)} %reshape.249), channel_id=1, replica_groups=mesh['item'=8,'code'=4] {'item'}, use_global_device_ids=true, to_apply=%region_15.16 | all-reduce | flops 8192 | bytes 65536 | tf_op jit(solution)/shard_map/pmax | solution.py:119
  403.7 33.0 %psum.59 = f32[8192]{0:T(1024)S(1)} all-reduce(f32[8192]{0:T(1024)S(1)} %exponential_multiply_fusion.2), channel_id=1, replica_groups=mesh['item'=8,'code'=4] {'item'}, use_global_device_ids=true, to_apply=%region_17.18 | all-reduce | flops 8192 | bytes 65536 | tf_op jit(solution)/shard_map/psum | solution.py:120
  437.5 1.0 gather_fusion.3
  438.6 7.6 %add_reduce_fusion.3 = f32[8,8,64]{2,1,0:T(8,128)S(1)} fusion(f32[8,8,8,64,64]{3,4,2,1,0:T(8,128)} %get-tuple-element.107, f32[8,8,8,64]{3,2,1,0:T(8,128)S(1)} %bitcast.101), kind=kLoop, calls=%fused_computation.37 | loop fusion | flops 4190208 | bytes 8536064 | tf_op jit(solution)/shard_map/reduce_max | solution.py:74
  446.2 7.6 %exponential_reduce_fusion.3 = f32[8,8,64]{2,1,0:T(8,128)S(1)} fusion(f32[8,8,8,64,64]{3,4,2,1,0:T(8,128)} %get-tuple-element.107, f32[8,8,64]{2,1,0:T(8,128)S(1)} %add_reduce_fusion.3, f32[8,8,8,64]{3,2,1,0:T(8,128)S(1)} %bitcast.102), kind=kLoop, calls=%fused_computation.31 | loop fusion | flops 6287360 | bytes 8552448 | tf_op jit(solution)/shard_map/reduce_sum | solution.py:75
  454.0 10.1 %pmax.44 = f32[4096]{0:T(1024)S(1)} all-reduce(f32[4096]{0:T(1024)S(1)} %reshape.254), channel_id=1, replica_groups=mesh['item'=8,'code'=4] {'code'}, use_global_device_ids=true, to_apply=%region_19.20 | all-reduce | flops 4096 | bytes 32768 | tf_op jit(solution)/shard_map/pmax | solution.py:81
  464.1 10.1 %psum.60 = f32[4096]{0:T(1024)S(1)} all-reduce(f32[4096]{0:T(1024)S(1)} %exponential_multiply_fusion.4), channel_id=1, replica_groups=mesh['item'=8,'code'=4] {'code'}, use_global_device_ids=true, to_apply=%region_21.22 | all-reduce | flops 4096 | bytes 32768 | tf_op jit(solution)/shard_map/psum | solution.py:82
  474.3 8.2 %add_reduce_fusion.2 = f32[8,8,8,64]{3,2,1,0:T(8,128)S(1)} fusion(f32[8,8,8,64,64]{3,4,2,1,0:T(8,128)} %get-tuple-element.107, f32[8,8,64]{2,1,0:T(8,128)S(1)} %add.175), kind=kLoop, calls=%fused_computation.36 | loop fusion | flops 4161536 | bytes 8536064 | tf_op jit(solution)/shard_map/reduce_max | solution.py:88
  482.5 11.1 %exponential_reduce_fusion.2 = f32[8,8,8,64]{3,2,1,0:T(8,128)S(1)} fusion(f32[8,8,8,64,64]{3,4,2,1,0:T(8,128)} %get-tuple-element.107, f32[8,8,8,64]{3,2,1,0:T(8,128)S(1)} %add_reduce_fusion.2, f32[8,8,64]{2,1,0:T(8,128)S(1)} %add.175), kind=kLoop, calls=%fused_computation.30 | loop fusion | flops 6258688 | bytes 8667136 | tf_op jit(solution)/shard_map/reduce_sum | solution.py:89
  493.6 6.7 while.45
  493.6 3.2 select_reduce_fusion.7
  497.0 3.2 select_reduce_fusion.7
  500.4 1.0 gather_fusion.4
  502.1 33.0 %pmax.45 = f32[8192]{0:T(1024)S(1)} all-reduce(f32[8192]{0:T(1024)S(1)} %reshape.256), channel_id=1, replica_groups=mesh['item'=8,'code'=4] {'item'}, use_global_device_ids=true, to_apply=%region_26.27 | all-reduce | flops 8192 | bytes 65536 | tf_op jit(solution)/shard_map/pmax | solution.py:119
  535.2 33.2 %psum.61 = f32[8192]{0:T(1024)S(1)} all-reduce(f32[8192]{0:T(1024)S(1)} %exponential_multiply_fusion.1), channel_id=1, replica_groups=mesh['item'=8,'code'=4] {'item'}, use_global_device_ids=true, to_apply=%region_28.29 | all-reduce | flops 8192 | bytes 65536 | tf_op jit(solution)/shard_map/psum | solution.py:120
  568.5 1.0 gather_fusion.5
  569.5 7.6 %add_reduce_fusion.1 = f32[8,8,64]{2,1,0:T(8,128)S(1)} fusion(f32[8,8,8,64,64]{3,4,2,1,0:T(8,128)} %get-tuple-element.107, f32[8,8,8,64]{3,2,1,0:T(8,128)S(1)} %bitcast.99), kind=kLoop, calls=%fused_computation.35 | loop fusion | flops 4190208 | bytes 8536064 | tf_op jit(solution)/shard_map/reduce_max | solution.py:74
  577.1 7.6 %exponential_reduce_fusion.1 = f32[8,8,64]{2,1,0:T(8,128)S(1)} fusion(f32[8,8,8,64,64]{3,4,2,1,0:T(8,128)} %get-tuple-element.107, f32[8,8,64]{2,1,0:T(8,128)S(1)} %add_reduce_fusion.1, f32[8,8,8,64]{3,2,1,0:T(8,128)S(1)} %bitcast.100), kind=kLoop, calls=%fused_computation.29 | loop fusion | flops 6287360 | bytes 8552448 | tf_op jit(solution)/shard_map/reduce_sum | solution.py:75
  584.9 10.1 %pmax.46 = f32[4096]{0:T(1024)S(1)} all-reduce(f32[4096]{0:T(1024)S(1)} %reshape.261), channel_id=1, replica_groups=mesh['item'=8,'code'=4] {'code'}, use_global_device_ids=true, to_apply=%region_30.31 | all-reduce | flops 4096 | bytes 32768 | tf_op jit(solution)/shard_map/pmax | solution.py:81
  595.0 10.1 %psum.62 = f32[4096]{0:T(1024)S(1)} all-reduce(f32[4096]{0:T(1024)S(1)} %exponential_multiply_fusion.3), channel_id=1, replica_groups=mesh['item'=8,'code'=4] {'code'}, use_global_device_ids=true, to_apply=%region_32.33 | all-reduce | flops 4096 | bytes 32768 | tf_op jit(solution)/shard_map/psum | solution.py:82
  605.2 8.2 %add_reduce_fusion = f32[8,8,8,64]{3,2,1,0:T(8,128)S(1)} fusion(f32[8,8,8,64,64]{3,4,2,1,0:T(8,128)} %get-tuple-element.107, f32[8,8,64]{2,1,0:T(8,128)S(1)} %add.183), kind=kLoop, calls=%fused_computation.34 | loop fusion | flops 4161536 | bytes 8536064 | tf_op jit(solution)/shard_map/reduce_max | solution.py:88
  613.5 11.1 %exponential_reduce_fusion = f32[8,8,8,64]{3,2,1,0:T(8,128)S(1)} fusion(f32[8,8,8,64,64]{3,4,2,1,0:T(8,128)} %get-tuple-element.107, f32[8,8,8,64]{3,2,1,0:T(8,128)S(1)} %add_reduce_fusion, f32[8,8,64]{2,1,0:T(8,128)S(1)} %add.183), kind=kLoop, calls=%fused_computation.28 | loop fusion | flops 6258688 | bytes 8667136 | tf_op jit(solution)/shard_map/reduce_sum | solution.py:89
  624.5 6.7 while.46
  624.6 3.2 select_reduce_fusion.8
  627.9 3.2 select_reduce_fusion.8
  631.4 1.0 gather_fusion.6
  633.1 33.0 %pmax.47 = f32[8192]{0:T(1024)S(1)} all-reduce(f32[8192]{0:T(1024)S(1)} %reshape.263), channel_id=1, replica_groups=mesh['item'=8,'code'=4] {'item'}, use_global_device_ids=true, to_apply=%region_37.38 | all-reduce | flops 8192 | bytes 65536 | tf_op jit(solution)/shard_map/pmax | solution.py:119
  666.1 33.0 %psum.63 = f32[8192]{0:T(1024)S(1)} all-reduce(f32[8192]{0:T(1024)S(1)} %exponential_multiply_fusion), channel_id=1, replica_groups=mesh['item'=8,'code'=4] {'item'}, use_global_device_ids=true, to_apply=%region_39.40 | all-reduce | flops 8192 | bytes 65536 | tf_op jit(solution)/shard_map/psum | solution.py:120
  (166 shorter events, 16.8 us)
Async XLA Ops:
  7.2 28.2 %copy-start = (s32[64,16]{0,1:T(8,128)S(1)}, s32[64,16]{0,1:T(8,128)}, u32[]{:S(2)}) copy-start(s32[64,16]{0,1:T(8,128)} %param.17) | copy-start | bytes 12292
  7.2 39.6 %all-gather.5.cloned.1.call-start = ((), (), s32[]{:S(2)}) async-start(), calls=%async_computation.1 | async-start | bytes 5242880 | tf_op jit(solution)/shard_map/all_gather | solution.py:14
  7.9 165.5 %all-gather.3.cloned.1.call-start = ((), (), s32[]{:S(2)}) async-start(), calls=%async_computation | async-start | bytes 9437184 | tf_op jit(solution)/shard_map/all_gather | solution.py:15
  35.4 4.6 copy-start.2
  302.9 10.7 %copy-start.1 = (f32[8,8,8,64,64]{3,4,2,1,0:T(8,128)S(1)}, f32[8,8,8,64,64]{3,4,2,1,0:T(8,128)}, u32[]{:S(2)}) copy-start(f32[8,8,8,64,64]{3,4,2,1,0:T(8,128)} %get-tuple-element.107) | copy-start | bytes 25165828
  302.9 37.6 %copy-start.3 = (f32[4096]{0:T(1024)S(1)}, f32[4096]{0:T(1024)}, u32[]{:S(2)}) copy-start(f32[4096]{0:T(1024)} %param.15) | copy-start | bytes 49156
  605.2 19.4 %copy-start.4 = (f32[4096]{0:T(1024)}, f32[4096]{0:T(1024)S(1)}, u32[]{:S(2)}) copy-start(f32[4096]{0:T(1024)S(1)} %add_subtract_fusion.3) | copy-start | bytes 49156
Sparse Core Ops, SparseCore 0:
  9.5 37.1 all-gather.4
  48.9 124.4 all-gather.2
where the time goes:
time: 708 us; the launch traced here: 707 us
  blocking collectives  286 us (40%)
  waiting for transfers between devices  127 us (18%)
  other arithmetic  127 us (18%)
  local copies, waits for them, and re-layouts  85.9 us (12%)
  matrix products  59.6 us (8%)
  between operations  15.8 us (2%)
    all_gather x1, waiting for transfers between devices, body(): code_cols = lax.all_gather(codebook, 'item', axis=0, tiled=True)  121 us
    pmax x3, blocking collectives, body(): joined_peak = lax.pmax(col_peak, 'item')  101 us
    psum x3, blocking collectives, body(): joined_total = lax.psum(col_total * jnp.exp(col_peak - joined_peak), 'item')  99.3 us
    dot_general x8, matrix products, build_tiles(): jnp.einsum('rbi,rbsj->bsij', own, picked, precision=lax.Precision.HIGHEST)  58.1 us
    gather x8, local copies, waits for them, and re-layouts, build_tiles(): picked = code_column_splits[:, ids, :]  49.4 us
    reduce_sum x3, other arithmetic, col_reduce(): block_total = jnp.sum(jnp.exp(logits - block_peak[:, :, None, :]), axis=2)  33.2 us
    psum x3, blocking collectives, body(): merged_total = lax.psum(row_total * jnp.exp(row_peak - merged_peak), 'code')  31.6 us
    pmax x3, blocking collectives, body(): merged_peak = lax.pmax(row_peak, 'code')  30.4 us
  transfers between devices with their start and end apart: 2, of which 2 were waited for; matrix products, arithmetic and copies ran while one was open for 2% of the time, Pallas kernels for 0%

commit v1 on v0

--- a/solution.py
+++ b/solution.py
@@ -117,7 +117,9 @@
         col_peak = col_peak.reshape(code_count)
         col_total = col_total.reshape(code_count)
         joined_peak = lax.pmax(col_peak, "item")
-        joined_total = lax.psum(col_total * jnp.exp(col_peak - joined_peak), "item")
+        block = col_total * jnp.exp(col_peak - joined_peak)
+        parts = lax.all_gather(block, "item")
+        joined_total = jnp.sum(parts, axis=0)
         code_potential = code_logmass - (joined_peak + jnp.log(joined_total))
     return (item_potential, code_potential)
 

time: 708 us -> 702 us (level)
    psum x3 -> x0, blocking collectives: 99.3 us -> none  [body(): joined_total = lax.psum(col_total * jnp.exp(col_peak - joined_peak), 'item')]
    all_gather x0 -> x3, blocking collectives: none -> 92.7 us  [body(): parts = lax.all_gather(block, 'item')]
where the time goes in v1:
time: 702 us; the launch traced here: 700 us
  blocking collectives  280 us (40%)
  waiting for transfers between devices  127 us (18%)
  other arithmetic  127 us (18%)
  local copies, waits for them, and re-layouts  86.1 us (12%)
  matrix products  59.6 us (8%)
  between operations  15.8 us (2%)
    all_gather x1, waiting for transfers between devices, body(): code_cols = lax.all_gather(codebook, 'item', axis=0, tiled=True)  121 us
    pmax x3, blocking collectives, body(): joined_peak = lax.pmax(col_peak, 'item')  101 us
    all_gather x3, blocking collectives, body(): parts = lax.all_gather(block, 'item')  92.7 us
    dot_general x8, matrix products, build_tiles(): jnp.einsum('rbi,rbsj->bsij', own, picked, precision=lax.Precision.HIGHEST)  58.1 us
    gather x8, local copies, waits for them, and re-layouts, build_tiles(): picked = code_column_splits[:, ids, :]  49.4 us
    reduce_sum x3, other arithmetic, col_reduce(): block_total = jnp.sum(jnp.exp(logits - block_peak[:, :, None, :]), axis=2)  33.2 us
    psum x3, blocking collectives, body(): merged_total = lax.psum(row_total * jnp.exp(row_peak - merged_peak), 'code')  31.6 us
    pmax x3, blocking collectives, body(): merged_peak = lax.pmax(row_peak, 'code')  30.4 us
  transfers between devices with their start and end apart: 2, of which 2 were waited for; matrix products, arithmetic and copies ran while one was open for 2% of the time, Pallas kernels for 0%

profile of v1, /device:TPU:0, one launch (start us, length us, event | category | flops | bytes accessed | tf_op | source)
XLA Modules:
  0.0 700.4 jit_solution(4799150685524247314)
XLA Ops:
  8.7 1.3 reduce_sum.99
  10.0 23.8 %psum.35 = f32[]{:T(128)} all-reduce(f32[]{:T(128)} %reduce_sum.99), channel_id=1, replica_groups=mesh['item'=8,'code'=4] {'item'}, use_global_device_ids=true, to_apply=%region_1.0 | all-reduce | flops 1 | bytes 8 | tf_op jit(solution)/shard_map/psum | solution.py:22
  35.4 3.9 gather_fusion.7
  41.4 1.0 gather_fusion.1
  42.6 4.1 all-gather.8.cloned.1.call-done
  46.8 5.6 copy.38
  52.4 121.0 %all-gather.6.cloned.1.call-done = f32[256,8192]{1,0:T(8,128)} async-done(((f32[32,8192]{1,0:T(8,128)}), f32[256,8192]{1,0:T(8,128)}) %all-gather.6.cloned.1.call-update) | async-done | bytes 8388624 | tf_op jit(solution)/shard_map/all_gather | solution.py:15
  173.4 9.0 %copy.37 = f32[256,8192]{0,1:T(8,128)} copy(f32[256,8192]{1,0:T(8,128)} %all-gather.6.cloned.1.call-done) | data formatting | bytes 16777216 | tf_op jit(solution)/shard_map/all_gather | solution.py:15
  182.4 120.6 %while.43 = (s32[]{:T(128)}, f32[8,8,8,64,64]{3,4,2,1,0:T(8,128)}, s32[8]{0:T(128)S(1)}, pred[64,8]{0,1:T(8,128)(4,1)S(1)}, s32[64,8]{0,1:T(8,128)S(1)}, /*index...) while((s32[]{:T(128)}, f32[8,8,8,64,64]{3,4,2,1,0:T(8,128)}, ...), condition=%wide.region_4.0_spmd, body=%wide.region_3.0_spmd.sunk | while | flops 805831872 | bytes 15212019 | solution.py:55
  183.9 6.2 gather_fusion
  190.2 7.3 %bitcast_dynamic-update-slice_fusion.2 = f32[8,8,8,64,64]{3,4,2,1,0:T(8,128)} fusion(f32[8,8,8,64,64]{3,4,2,1,0:T(8,128)} %get-tuple-element.349, s32[]{:T(128)} %get-tuple-element.348, f32[256,8,8,64]{0,3,2,1:T(8,128)} %bitcast.88, pred[8,8]{1,0:T(8,128)(4,1)S(1)} %copy.63, f32[256,64,64]{0,2,1:T(8,128)} %get-tuple-element.365, s32[]{:T(128)S(6)} %select_n.148), kind=kOutput, calls=%fused_computation.8.clone.1 | convolution fusion | flops 805830656 | bytes 6816324 | tf_op jit(solution)/shard_map/while/body/eval_jaxpr/rbi,rbsj->bsij/dot_general | solution.py:41
  199.0 6.2 gather_fusion
  205.3 7.2 %bitcast_dynamic-update-slice_fusion.2 = f32[8,8,8,64,64]{3,4,2,1,0:T(8,128)} fusion(f32[8,8,8,64,64]{3,4,2,1,0:T(8,128)} %get-tuple-element.349, s32[]{:T(128)} %get-tuple-element.348, f32[256,8,8,64]{0,3,2,1:T(8,128)} %bitcast.88, pred[8,8]{1,0:T(8,128)(4,1)S(1)} %copy.63, f32[256,64,64]{0,2,1:T(8,128)} %get-tuple-element.365, s32[]{:T(128)S(6)} %select_n.148), kind=kOutput, calls=%fused_computation.8.clone.1 | convolution fusion | flops 805830656 | bytes 6816324 | tf_op jit(solution)/shard_map/while/body/eval_jaxpr/rbi,rbsj->bsij/dot_general | solution.py:41
  214.0 6.2 gather_fusion
  220.3 7.3 %bitcast_dynamic-update-slice_fusion.2 = f32[8,8,8,64,64]{3,4,2,1,0:T(8,128)} fusion(f32[8,8,8,64,64]{3,4,2,1,0:T(8,128)} %get-tuple-element.349, s32[]{:T(128)} %get-tuple-element.348, f32[256,8,8,64]{0,3,2,1:T(8,128)} %bitcast.88, pred[8,8]{1,0:T(8,128)(4,1)S(1)} %copy.63, f32[256,64,64]{0,2,1:T(8,128)} %get-tuple-element.365, s32[]{:T(128)S(6)} %select_n.148), kind=kOutput, calls=%fused_computation.8.clone.1 | convolution fusion | flops 805830656 | bytes 6816324 | tf_op jit(solution)/shard_map/while/body/eval_jaxpr/rbi,rbsj->bsij/dot_general | solution.py:41
  229.0 6.2 gather_fusion
  235.4 7.3 %bitcast_dynamic-update-slice_fusion.2 = f32[8,8,8,64,64]{3,4,2,1,0:T(8,128)} fusion(f32[8,8,8,64,64]{3,4,2,1,0:T(8,128)} %get-tuple-element.349, s32[]{:T(128)} %get-tuple-element.348, f32[256,8,8,64]{0,3,2,1:T(8,128)} %bitcast.88, pred[8,8]{1,0:T(8,128)(4,1)S(1)} %copy.63, f32[256,64,64]{0,2,1:T(8,128)} %get-tuple-element.365, s32[]{:T(128)S(6)} %select_n.148), kind=kOutput, calls=%fused_computation.8.clone.1 | convolution fusion | flops 805830656 | bytes 6816324 | tf_op jit(solution)/shard_map/while/body/eval_jaxpr/rbi,rbsj->bsij/dot_general | solution.py:41
  244.1 6.2 gather_fusion
  250.4 7.3 %bitcast_dynamic-update-slice_fusion.2 = f32[8,8,8,64,64]{3,4,2,1,0:T(8,128)} fusion(f32[8,8,8,64,64]{3,4,2,1,0:T(8,128)} %get-tuple-element.349, s32[]{:T(128)} %get-tuple-element.348, f32[256,8,8,64]{0,3,2,1:T(8,128)} %bitcast.88, pred[8,8]{1,0:T(8,128)(4,1)S(1)} %copy.63, f32[256,64,64]{0,2,1:T(8,128)} %get-tuple-element.365, s32[]{:T(128)S(6)} %select_n.148), kind=kOutput, calls=%fused_computation.8.clone.1 | convolution fusion | flops 805830656 | bytes 6816324 | tf_op jit(solution)/shard_map/while/body/eval_jaxpr/rbi,rbsj->bsij/dot_general | solution.py:41
  259.2 6.2 gather_fusion
  265.6 7.2 %bitcast_dynamic-update-slice_fusion.2 = f32[8,8,8,64,64]{3,4,2,1,0:T(8,128)} fusion(f32[8,8,8,64,64]{3,4,2,1,0:T(8,128)} %get-tuple-element.349, s32[]{:T(128)} %get-tuple-element.348, f32[256,8,8,64]{0,3,2,1:T(8,128)} %bitcast.88, pred[8,8]{1,0:T(8,128)(4,1)S(1)} %copy.63, f32[256,64,64]{0,2,1:T(8,128)} %get-tuple-element.365, s32[]{:T(128)S(6)} %select_n.148), kind=kOutput, calls=%fused_computation.8.clone.1 | convolution fusion | flops 805830656 | bytes 6816324 | tf_op jit(solution)/shard_map/while/body/eval_jaxpr/rbi,rbsj->bsij/dot_general | solution.py:41
  274.3 6.2 gather_fusion
  280.6 7.3 %bitcast_dynamic-update-slice_fusion.2 = f32[8,8,8,64,64]{3,4,2,1,0:T(8,128)} fusion(f32[8,8,8,64,64]{3,4,2,1,0:T(8,128)} %get-tuple-element.349, s32[]{:T(128)} %get-tuple-element.348, f32[256,8,8,64]{0,3,2,1:T(8,128)} %bitcast.88, pred[8,8]{1,0:T(8,128)(4,1)S(1)} %copy.63, f32[256,64,64]{0,2,1:T(8,128)} %get-tuple-element.365, s32[]{:T(128)S(6)} %select_n.148), kind=kOutput, calls=%fused_computation.8.clone.1 | convolution fusion | flops 805830656 | bytes 6816324 | tf_op jit(solution)/shard_map/while/body/eval_jaxpr/rbi,rbsj->bsij/dot_general | solution.py:41
  289.4 6.2 gather_fusion
  295.7 7.3 %bitcast_dynamic-update-slice_fusion.2 = f32[8,8,8,64,64]{3,4,2,1,0:T(8,128)} fusion(f32[8,8,8,64,64]{3,4,2,1,0:T(8,128)} %get-tuple-element.349, s32[]{:T(128)} %get-tuple-element.348, f32[256,8,8,64]{0,3,2,1:T(8,128)} %bitcast.88, pred[8,8]{1,0:T(8,128)(4,1)S(1)} %copy.63, f32[256,64,64]{0,2,1:T(8,128)} %get-tuple-element.365, s32[]{:T(128)S(6)} %select_n.148), kind=kOutput, calls=%fused_computation.8.clone.1 | convolution fusion | flops 805830656 | bytes 6816324 | tf_op jit(solution)/shard_map/while/body/eval_jaxpr/rbi,rbsj->bsij/dot_general | solution.py:41
  302.9 9.4 %add_reduce_fusion.5 = f32[8,8,64]{2,1,0:T(8,128)S(1)} fusion(f32[8,8,8,64,64]{3,4,2,1,0:T(8,128)} %get-tuple-element.107, f32[8,8,8,64]{3,2,1,0:T(8,128)S(1)} %bitcast.97), kind=kLoop, calls=%fused_computation.39 | loop fusion | flops 4190208 | bytes 8536064 | tf_op jit(solution)/shard_map/reduce_max | solution.py:74
  312.3 1.3 copy-done.1
  313.7 5.1 exponential_reduce_fusion.5
  319.0 10.2 %pmax.42 = f32[4096]{0:T(1024)S(1)} all-reduce(f32[4096]{0:T(1024)S(1)} %reshape.247), channel_id=1, replica_groups=mesh['item'=8,'code'=4] {'code'}, use_global_device_ids=true, to_apply=%region_8.9 | all-reduce | flops 4096 | bytes 32768 | tf_op jit(solution)/shard_map/pmax | solution.py:81
  329.2 11.4 %all-reduce.3 = (f32[4096]{0:T(1024)S(1)}, f32[]{:T(128)}) all-reduce(f32[4096]{0:T(1024)S(1)} %exponential_multiply_fusion.5, f32[]{:T(128)} %reduce_sum.100), channel_id=1, replica_groups=mesh['item'=8,'code'=4] {'code'}, use_global_device_ids=true, to_apply=%region_10.11 | all-reduce | flops 4097 | bytes 32776 | tf_op jit(solution)/shard_map/psum | solution.py:82
  340.7 8.2 %add_reduce_fusion.4 = f32[8,8,8,64]{3,2,1,0:T(8,128)S(1)} fusion(f32[8,8,8,64,64]{3,4,2,1,0:T(8,128)} %get-tuple-element.107, f32[8,8,64]{2,1,0:T(8,128)S(1)} %add.160), kind=kLoop, calls=%fused_computation.38 | loop fusion | flops 4161536 | bytes 8536064 | tf_op jit(solution)/shard_map/reduce_max | solution.py:88
  348.9 11.1 %exponential_reduce_fusion.4 = f32[8,8,8,64]{3,2,1,0:T(8,128)S(1)} fusion(f32[8,8,8,64,64]{3,4,2,1,0:T(8,128)} %get-tuple-element.107, f32[8,8,8,64]{3,2,1,0:T(8,128)S(1)} %add_reduce_fusion.4, f32[8,8,64]{2,1,0:T(8,128)S(1)} %add.160), kind=kLoop, calls=%fused_computation.32 | loop fusion | flops 6258688 | bytes 8667136 | tf_op jit(solution)/shard_map/reduce_sum | solution.py:89
  359.9 6.7 while.44
  360.0 3.2 select_reduce_fusion.6
  363.3 3.2 select_reduce_fusion.6
  366.8 1.0 gather_fusion.2
  368.5 35.2 %pmax.43 = f32[8192]{0:T(1024)S(1)} all-reduce(f32[8192]{0:T(1024)S(1)} %reshape.249), channel_id=1, replica_groups=mesh['item'=8,'code'=4] {'item'}, use_global_device_ids=true, to_apply=%region_15.16 | all-reduce | flops 8192 | bytes 65536 | tf_op jit(solution)/shard_map/pmax | solution.py:119
  403.7 30.7 %all-gather = f32[65536]{0:T(1024)S(1)} all-gather(f32[8192]{0:T(1024)S(1)} %exponential_multiply_fusion.2), channel_id=2, replica_groups=mesh['item'=8,'code'=4] {'item'}, dimensions={0}, use_global_device_ids=true | all-gather | bytes 294912 | tf_op jit(solution)/shard_map/all_gather | solution.py:121
  435.4 1.0 gather_fusion.3
  436.4 7.6 %add_reduce_fusion.3 = f32[8,8,64]{2,1,0:T(8,128)S(1)} fusion(f32[8,8,8,64,64]{3,4,2,1,0:T(8,128)} %get-tuple-element.107, f32[8,8,8,64]{3,2,1,0:T(8,128)S(1)} %bitcast.101), kind=kLoop, calls=%fused_computation.37 | loop fusion | flops 4190208 | bytes 8536064 | tf_op jit(solution)/shard_map/reduce_max | solution.py:74
  444.0 7.6 %exponential_reduce_fusion.3 = f32[8,8,64]{2,1,0:T(8,128)S(1)} fusion(f32[8,8,8,64,64]{3,4,2,1,0:T(8,128)} %get-tuple-element.107, f32[8,8,64]{2,1,0:T(8,128)S(1)} %add_reduce_fusion.3, f32[8,8,8,64]{3,2,1,0:T(8,128)S(1)} %bitcast.102), kind=kLoop, calls=%fused_computation.31 | loop fusion | flops 6287360 | bytes 8552448 | tf_op jit(solution)/shard_map/reduce_sum | solution.py:75
  451.8 10.1 %pmax.44 = f32[4096]{0:T(1024)S(1)} all-reduce(f32[4096]{0:T(1024)S(1)} %reshape.254), channel_id=1, replica_groups=mesh['item'=8,'code'=4] {'code'}, use_global_device_ids=true, to_apply=%region_19.20 | all-reduce | flops 4096 | bytes 32768 | tf_op jit(solution)/shard_map/pmax | solution.py:81
  461.9 10.1 %psum.38 = f32[4096]{0:T(1024)S(1)} all-reduce(f32[4096]{0:T(1024)S(1)} %exponential_multiply_fusion.4), channel_id=1, replica_groups=mesh['item'=8,'code'=4] {'code'}, use_global_device_ids=true, to_apply=%region_21.22 | all-reduce | flops 4096 | bytes 32768 | tf_op jit(solution)/shard_map/psum | solution.py:82
  472.1 8.2 %add_reduce_fusion.2 = f32[8,8,8,64]{3,2,1,0:T(8,128)S(1)} fusion(f32[8,8,8,64,64]{3,4,2,1,0:T(8,128)} %get-tuple-element.107, f32[8,8,64]{2,1,0:T(8,128)S(1)} %add.169), kind=kLoop, calls=%fused_computation.36 | loop fusion | flops 4161536 | bytes 8536064 | tf_op jit(solution)/shard_map/reduce_max | solution.py:88
  480.4 11.1 %exponential_reduce_fusion.2 = f32[8,8,8,64]{3,2,1,0:T(8,128)S(1)} fusion(f32[8,8,8,64,64]{3,4,2,1,0:T(8,128)} %get-tuple-element.107, f32[8,8,8,64]{3,2,1,0:T(8,128)S(1)} %add_reduce_fusion.2, f32[8,8,64]{2,1,0:T(8,128)S(1)} %add.169), kind=kLoop, calls=%fused_computation.30 | loop fusion | flops 6258688 | bytes 8667136 | tf_op jit(solution)/shard_map/reduce_sum | solution.py:89
  491.4 6.7 while.45
  491.5 3.2 select_reduce_fusion.7
  494.8 3.2 select_reduce_fusion.7
  498.3 1.0 gather_fusion.4
  500.0 33.0 %pmax.45 = f32[8192]{0:T(1024)S(1)} all-reduce(f32[8192]{0:T(1024)S(1)} %reshape.256), channel_id=1, replica_groups=mesh['item'=8,'code'=4] {'item'}, use_global_device_ids=true, to_apply=%region_26.27 | all-reduce | flops 8192 | bytes 65536 | tf_op jit(solution)/shard_map/pmax | solution.py:119
  533.0 31.1 %all-gather.1 = f32[65536]{0:T(1024)S(1)} all-gather(f32[8192]{0:T(1024)S(1)} %exponential_multiply_fusion.1), channel_id=3, replica_groups=mesh['item'=8,'code'=4] {'item'}, dimensions={0}, use_global_device_ids=true | all-gather | bytes 294912 | tf_op jit(solution)/shard_map/all_gather | solution.py:121
  564.3 1.0 gather_fusion.5
  565.3 7.6 %add_reduce_fusion.1 = f32[8,8,64]{2,1,0:T(8,128)S(1)} fusion(f32[8,8,8,64,64]{3,4,2,1,0:T(8,128)} %get-tuple-element.107, f32[8,8,8,64]{3,2,1,0:T(8,128)S(1)} %bitcast.99), kind=kLoop, calls=%fused_computation.35 | loop fusion | flops 4190208 | bytes 8536064 | tf_op jit(solution)/shard_map/reduce_max | solution.py:74
  572.9 7.6 %exponential_reduce_fusion.1 = f32[8,8,64]{2,1,0:T(8,128)S(1)} fusion(f32[8,8,8,64,64]{3,4,2,1,0:T(8,128)} %get-tuple-element.107, f32[8,8,64]{2,1,0:T(8,128)S(1)} %add_reduce_fusion.1, f32[8,8,8,64]{3,2,1,0:T(8,128)S(1)} %bitcast.100), kind=kLoop, calls=%fused_computation.29 | loop fusion | flops 6287360 | bytes 8552448 | tf_op jit(solution)/shard_map/reduce_sum | solution.py:75
  580.7 10.1 %pmax.46 = f32[4096]{0:T(1024)S(1)} all-reduce(f32[4096]{0:T(1024)S(1)} %reshape.261), channel_id=1, replica_groups=mesh['item'=8,'code'=4] {'code'}, use_global_device_ids=true, to_apply=%region_30.31 | all-reduce | flops 4096 | bytes 32768 | tf_op jit(solution)/shard_map/pmax | solution.py:81
  590.8 10.1 %psum.39 = f32[4096]{0:T(1024)S(1)} all-reduce(f32[4096]{0:T(1024)S(1)} %exponential_multiply_fusion.3), channel_id=1, replica_groups=mesh['item'=8,'code'=4] {'code'}, use_global_device_ids=true, to_apply=%region_32.33 | all-reduce | flops 4096 | bytes 32768 | tf_op jit(solution)/shard_map/psum | solution.py:82
  601.1 8.2 %add_reduce_fusion = f32[8,8,8,64]{3,2,1,0:T(8,128)S(1)} fusion(f32[8,8,8,64,64]{3,4,2,1,0:T(8,128)} %get-tuple-element.107, f32[8,8,64]{2,1,0:T(8,128)S(1)} %add.177), kind=kLoop, calls=%fused_computation.34 | loop fusion | flops 4161536 | bytes 8536064 | tf_op jit(solution)/shard_map/reduce_max | solution.py:88
  609.3 11.1 %exponential_reduce_fusion = f32[8,8,8,64]{3,2,1,0:T(8,128)S(1)} fusion(f32[8,8,8,64,64]{3,4,2,1,0:T(8,128)} %get-tuple-element.107, f32[8,8,8,64]{3,2,1,0:T(8,128)S(1)} %add_reduce_fusion, f32[8,8,64]{2,1,0:T(8,128)S(1)} %add.177), kind=kLoop, calls=%fused_computation.28 | loop fusion | flops 6258688 | bytes 8667136 | tf_op jit(solution)/shard_map/reduce_sum | solution.py:89
  620.4 6.7 while.46
  620.4 3.2 select_reduce_fusion.8
  623.7 3.2 select_reduce_fusion.8
  627.2 1.0 gather_fusion.6
  628.9 33.0 %pmax.47 = f32[8192]{0:T(1024)S(1)} all-reduce(f32[8192]{0:T(1024)S(1)} %reshape.263), channel_id=1, replica_groups=mesh['item'=8,'code'=4] {'item'}, use_global_device_ids=true, to_apply=%region_37.38 | all-reduce | flops 8192 | bytes 65536 | tf_op jit(solution)/shard_map/pmax | solution.py:119
  661.9 30.9 %all-gather.2 = f32[65536]{0:T(1024)S(1)} all-gather(f32[8192]{0:T(1024)S(1)} %exponential_multiply_fusion), channel_id=4, replica_groups=mesh['item'=8,'code'=4] {'item'}, dimensions={0}, use_global_device_ids=true | all-gather | bytes 294912 | tf_op jit(solution)/shard_map/all_gather | solution.py:121
  (172 shorter events, 17.2 us)
Async XLA Ops:
  7.2 28.2 %copy-start = (s32[64,16]{0,1:T(8,128)S(1)}, s32[64,16]{0,1:T(8,128)}, u32[]{:S(2)}) copy-start(s32[64,16]{0,1:T(8,128)} %param.17) | copy-start | bytes 12292
  7.2 39.6 %all-gather.8.cloned.1.call-start = ((), (), s32[]{:S(2)}) async-start(), calls=%async_computation.1 | async-start | bytes 5242880 | tf_op jit(solution)/shard_map/all_gather | solution.py:14
  7.9 165.5 %all-gather.6.cloned.1.call-start = ((), (), s32[]{:S(2)}) async-start(), calls=%async_computation | async-start | bytes 9437184 | tf_op jit(solution)/shard_map/all_gather | solution.py:15
  35.4 4.6 copy-start.2
  302.9 10.7 %copy-start.1 = (f32[8,8,8,64,64]{3,4,2,1,0:T(8,128)S(1)}, f32[8,8,8,64,64]{3,4,2,1,0:T(8,128)}, u32[]{:S(2)}) copy-start(f32[8,8,8,64,64]{3,4,2,1,0:T(8,128)} %get-tuple-element.107) | copy-start | bytes 25165828
  302.9 37.6 %copy-start.3 = (f32[4096]{0:T(1024)S(1)}, f32[4096]{0:T(1024)}, u32[]{:S(2)}) copy-start(f32[4096]{0:T(1024)} %param.15) | copy-start | bytes 49156
  601.0 19.4 %copy-start.4 = (f32[4096]{0:T(1024)}, f32[4096]{0:T(1024)S(1)}, u32[]{:S(2)}) copy-start(f32[4096]{0:T(1024)S(1)} %add_subtract_fusion.3) | copy-start | bytes 49156
Sparse Core Ops, SparseCore 0:
  9.5 37.1 all-gather.7
  48.9 124.4 all-gather.5
